TPU v7x, 32 devices: a whole 2x2x4 slice. The times are simulated.
32 devices in a mesh: chan: 4 (over y, x), blk: 8 (over z, core).
Axes of the slice: x: 2, y: 2, z: 4, core: 2. Of those that a mesh axis runs over, the one named last changes fastest.
Arguments:
- coeffs: bfloat16 [12, 2, 3072, 1536], P('chan', None, 'blk'), may hold values from -0.15 to 0.15
- legendre: bfloat16 [4, 768, 256, 1536], P('chan', 'blk'), may hold values from -0.15625 to 0.15625
- m_order: int32 [3072], replicated, may hold values from 0 to 3071, as said below
- sector_len: int32 [512, 16], P(('chan', 'blk')), may hold values from 256 to 4352, as said below
Outputs:
- ilc_map: float32 [512, 8192], P(('chan', 'blk'))
Inputs may be any that keep to these rules, and one draw needn't show every extreme that they name: `m_order`: a permutation of 0 to 3071; slots 2 j and 2 j + 1 hold the orders m and 3071 - m. `sector_len`: the 16 lengths of each cycle sum to 8192.
All inputs are finite; a program needn't handle non-finite values.
Results may differ from a plain program's by a relative error of at most 0.0003.
Values may be sent and summed in bfloat16 or wider, within the bound.
A program may use at most 512 MiB of HBM per device.

v0:
```python
import jax
import jax.numpy as jnp
from jax import lax
from jax.sharding import PartitionSpec as P

M = 3072
LB = 1536
PIX = 8192
RIDGE_FACTOR = 0.05
TWO_PI = 6.283185307179586


def cycle_synthesis(spectra, orders):
    highest = lax.Precision.HIGHEST
    order_count = spectra.shape[-1]
    fine_count = 128
    coarse_count = PIX // fine_count
    coarse_phase = (lax.iota(jnp.int32, coarse_count) * fine_count)[:, None] * orders[None, :] % PIX
    fine_phase = orders[:, None] * lax.iota(jnp.int32, fine_count)[None, :] % PIX
    coarse_angle = coarse_phase.astype(jnp.float32) * (TWO_PI / PIX)
    fine_angle = fine_phase.astype(jnp.float32) * (TWO_PI / PIX)
    weight = jnp.where(orders == 0, 1.0, 2.0).astype(jnp.float32)
    coarse_cos = jnp.cos(coarse_angle)
    coarse_sin = jnp.sin(coarse_angle)
    fine_cos = weight[:, None] * jnp.cos(fine_angle)
    fine_sin = weight[:, None] * jnp.sin(fine_angle)
    real_part = spectra[:, 0].reshape(-1, 1, order_count)
    imag_part = spectra[:, 1].reshape(-1, 1, order_count)
    shifted_real = (real_part * coarse_cos[None] - imag_part * coarse_sin[None]).reshape(
        -1, order_count
    )
    shifted_imag = (real_part * coarse_sin[None] + imag_part * coarse_cos[None]).reshape(
        -1, order_count
    )
    result = jnp.dot(shifted_real, fine_cos, precision=highest, preferred_element_type=jnp.float32)
    result = result - jnp.dot(
        shifted_imag, fine_sin, precision=highest, preferred_element_type=jnp.float32
    )
    return result.reshape(spectra.shape[0], spectra.shape[2], PIX)


def cycle_combine(cycle_map, lengths):
    highest = lax.Precision.HIGHEST
    channel_count = cycle_map.shape[0]
    sector_end = jnp.cumsum(lengths)
    sector_start = sector_end - lengths
    pixels = lax.iota(jnp.int32, PIX)
    member = (
        (pixels[None, :] >= sector_start[:, None]) & (pixels[None, :] < sector_end[:, None])
    ).astype(jnp.float32)
    products = (cycle_map[:, None, :] * cycle_map[None, :, :]).reshape(
        channel_count * channel_count, PIX
    )
    moments = jnp.einsum("qx,kx->kq", products, member, precision=highest)
    covariance = (
        moments.reshape(-1, channel_count, channel_count)
        / lengths.astype(jnp.float32)[:, None, None]
    )
    trace_part = jnp.trace(covariance, axis1=1, axis2=2) * (RIDGE_FACTOR / channel_count)
    regular = covariance + trace_part[:, None, None] * jnp.eye(channel_count, dtype=jnp.float32)
    factor = jnp.linalg.cholesky(regular)
    unit_rhs = jnp.ones((covariance.shape[0], channel_count, 1), jnp.float32)
    forward = lax.linalg.triangular_solve(factor, unit_rhs, left_side=True, lower=True)
    solved = lax.linalg.triangular_solve(
        factor, forward, left_side=True, lower=True, transpose_a=True
    )[:, :, 0]
    weights = solved / jnp.sum(solved, axis=1, keepdims=True)
    pixel_weights = jnp.einsum("ka,kx->ax", weights, member, precision=highest)
    return jnp.sum(pixel_weights * cycle_map, axis=0)


def per_device(coeffs, legendre, m_order, sector_len):
    slot_count = legendre.shape[1]
    group_count = lax.axis_size("chan")
    block_count = lax.axis_size("blk")
    first_slot = (lax.axis_index("blk") * group_count + lax.axis_index("chan")) * slot_count
    orders = lax.dynamic_slice_in_dim(m_order, first_slot, slot_count, 0)
    operator = legendre[0]
    degree = M - LB + lax.iota(jnp.int32, LB)
    valid_mask = degree[None, :] >= orders[:, None]
    zero_value = jnp.zeros((), coeffs.dtype)
    coeff_part = lax.all_to_all(coeffs, "chan", split_axis=2, concat_axis=0, tiled=True)
    odd_mask = (degree[None, :] + orders[:, None]) % 2 == 1
    even_part = jnp.where((valid_mask & ~odd_mask)[None, None], coeff_part, zero_value)
    odd_part = jnp.where((valid_mask & odd_mask)[None, None], coeff_part, zero_value)
    even_sum = jnp.einsum("cpsl,srl->cprs", even_part, operator, preferred_element_type=jnp.float32)
    odd_sum = jnp.einsum("cpsl,srl->cprs", odd_part, operator, preferred_element_type=jnp.float32)
    spectra = jnp.concatenate([even_sum + odd_sum, even_sum - odd_sum], axis=2)
    order_joined = (
        m_order.reshape(block_count, group_count, slot_count).transpose(1, 0, 2).reshape(-1)
    )
    cycle_maps = (lambda spectrum: cycle_synthesis(spectrum, order_joined))(
        lax.all_to_all(spectra, ("chan", "blk"), split_axis=2, concat_axis=3, tiled=True)
    )
    return lax.map(
        lambda cycle_pair: cycle_combine(cycle_pair[0], cycle_pair[1]),
        (jnp.moveaxis(cycle_maps, 1, 0), sector_len),
    )


def solution(mesh):
    placed = (
        P("chan", None, "blk", None),
        P("chan", "blk", None, None),
        P(),
        P(("chan", "blk"), None),
    )
    return jax.shard_map(
        per_device, mesh=mesh, in_specs=placed, out_specs=P(("chan", "blk"), None), check_vma=False
    )
```

profile of v0, /device:TPU:0, one launch (start us, length us, event | category | flops | bytes accessed | tf_op | source)
XLA Modules:
  0.0 1442.0 jit_solution(16301609392654005439)
XLA Ops:
  0.0 11.6 copy.69
  11.6 5.9 all-to-all-start
  18.2 104.5 %all-to-all-done = bf16[3,2,384,1536]{3,0,1,2:T(4,128)(2,1)} async-done(((bf16[3,2,384,1536]{3,0,1,2:T(4,128)(2,1)}), bf16[3,2,384,1536]{3,0,1,2:T(4,128)(2,1)}, u32[]{:S(2)}, u32[]{:S(2)}) %all-to-all-start) | async-done | bytes 7077920 | tf_op jit(solution)/shard_map/all_to_all | solution.py:82
  122.7 6.5 copy.70
  129.2 3.4 copy.71
  132.6 10.2 bitcast_select_fusion
  142.8 33.3 %fusion.23 = f32[96,12,2,256]{3,1,2,0:T(8,128)S(1)} fusion(bf16[1,96,256,1536]{3,2,1,0:T(8,128)(2,1)} %param.7, bf16[12,2,96,1536]{3,2,1,0:T(8,128)(2,1)} %get-tuple-element.40), kind=kOutput, calls=%fused_computation.41 | convolution fusion | flops 1811939328 | bytes 84934656 | tf_op jit(solution)/shard_map/cpsl,srl->cprs/dot_general | solution.py:87
  176.1 34.2 %add_bitcast_fusion = (f32[12,2,256,96]{2,0,1,3:T(8,128)}, f32[12,2,256,96]{2,0,1,3:T(8,128)}) fusion(f32[96,12,2,256]{3,1,2,0:T(8,128)S(1)} %fusion.23, bf16[1,96,256,1536]{3,2,1,0:T(8,128)(2,1)} %param.7, bf16[12,2,96,1536]{3,2,1,0:T(8,128)(2,1)} %get-tuple-element.41), kind=kOutput, calls=%fused_computation.53 | convolution fusion | flops 1813118976 | bytes 89653248 | tf_op jit(solution)/shard_map/cpsl,srl->cprs/dot_general | solution.py:86
  210.3 6.7 pad_maximum_fusion
  217.0 9.7 copy.74
  226.7 5.2 all-to-all-start.1
  232.1 4.2 fusion.50
  236.3 8.1 fusion.76
  244.4 8.1 fusion.74
  252.4 119.3 %all-to-all-done.1 = f32[12,2,512,96]{3,1,0,2:T(2,128)} async-done(((f32[12,2,512,96]{3,1,0,2:T(2,128)}), f32[12,2,512,96]{3,1,0,2:T(2,128)}, u32[]{:S(2)}, u32[]{:S(2)}) %all-to-all-start.1) | async-done | bytes 4718624 | tf_op jit(solution)/shard_map/all_to_all | solution.py:93
  371.8 4.0 copy.75
  375.8 5.0 copy.76
  380.8 7.7 all_to_all.33
  391.4 95.4 %multiply_add_fusion = (f32[192,64,3072]{2,1,0:T(8,128)}, f32[192,64,3072]{2,1,0:T(8,128)}) fusion(f32[64,3072]{1,0:T(8,128)} %get-tuple-element.49, f32[192,3072]{1,0:T(8,128)S(1)} %bitcast.106, f32[64,3072]{1,0:T(8,128)} %get-tuple-element.48, f32[192,3072]{1,0:T(8,128)S(1)} %bitcast.105), kind=kLoop, calls=%fused_computation.39 | loop fusion | flops 226492416 | bytes 308281344 | tf_op jit(solution)/shard_map/add | solution.py:32
  486.8 126.1 %fusion.34 = f32[12288,128]{1,0:T(8,128)} fusion(f32[12288,3072]{1,0:T(8,128)} %bitcast.29, f32[3072,128]{1,0:T(8,128)} %fusion.76), kind=kOutput, calls=%fused_computation.62 | convolution fusion | flops 57982058496 | bytes 158859264 | tf_op jit(solution)/shard_map/dot_general | solution.py:35
  612.9 125.4 %convolution_subtract_fusion = f32[12288,128]{1,0:T(8,128)} fusion(f32[12288,128]{1,0:T(8,128)} %fusion.34, f32[12288,3072]{1,0:T(8,128)} %bitcast.30, f32[3072,128]{1,0:T(8,128)S(1)} %copy-done), kind=kOutput, calls=%fused_computation.45 | convolution fusion | flops 57983631360 | bytes 165150720 | tf_op jit(solution)/shard_map/dot_general | solution.py:36
  738.3 7.4 reshape.296
  745.7 9.7 copy.91
  755.4 686.4 %while.10 = (s32[]{:T(128)}, f32[16,8192]{1,0:T(8,128)}, s32[16,16]{1,0:T(8,128)}, f32[16,12,8192]{2,1,0:T(8,128)}, s32[]{:T(128)}, /*index=5*/s32[]{:T(128)}, f32[]{:T(128)}, f32[]{:T(128)}) while((s32[]{:T(128)}, f32[16,8192]{1,0:T(8,128)}, s32[16,16]{1,0:T(8,128)}, f32[16,12,8192]{2,1,0:T(8,128)}, s32[]{:T(128)}, /*index=5*/s32[]{:T(128)}, ...), condition=%wide.region_7.8_spmd, body=%wide.region_0.7_spmd.sunk | while | flops 247610512 | bytes 1840549 | solution.py:95
  762.4 17.6 %custom-call.12 = f32[16,12,12]{2,1,0:T(8,128)S(1)} custom-call(f32[16,12,12]{2,1,0:T(8,128)S(1)} %copy.101), custom_call_target="Cholesky" | custom-call | tf_op jit(solution)/shard_map/while/body/eval_jaxpr/jit(cholesky)/cholesky | solution.py:61
  780.3 14.9 %custom-call.13 = f32[16,1,12,12]{2,3,1,0:T(8,128)S(1)} custom-call(f32[16,1,12,12]{3,2,1,0:T(8,128)S(1)} %select_bitcast_fusion.2), custom_call_target="InvertDiagBlocksLowerTriangular" | custom-call | tf_op jit(solution)/shard_map/while/body/eval_jaxpr/triangular_solve | solution.py:64
  801.0 3.2 fusion.100
  805.3 17.6 %custom-call.12 = f32[16,12,12]{2,1,0:T(8,128)S(1)} custom-call(f32[16,12,12]{2,1,0:T(8,128)S(1)} %copy.101), custom_call_target="Cholesky" | custom-call | tf_op jit(solution)/shard_map/while/body/eval_jaxpr/jit(cholesky)/cholesky | solution.py:61
  823.2 14.9 %custom-call.13 = f32[16,1,12,12]{2,3,1,0:T(8,128)S(1)} custom-call(f32[16,1,12,12]{3,2,1,0:T(8,128)S(1)} %select_bitcast_fusion.2), custom_call_target="InvertDiagBlocksLowerTriangular" | custom-call | tf_op jit(solution)/shard_map/while/body/eval_jaxpr/triangular_solve | solution.py:64
  848.2 17.6 %custom-call.12 = f32[16,12,12]{2,1,0:T(8,128)S(1)} custom-call(f32[16,12,12]{2,1,0:T(8,128)S(1)} %copy.101), custom_call_target="Cholesky" | custom-call | tf_op jit(solution)/shard_map/while/body/eval_jaxpr/jit(cholesky)/cholesky | solution.py:61
  866.1 14.9 %custom-call.13 = f32[16,1,12,12]{2,3,1,0:T(8,128)S(1)} custom-call(f32[16,1,12,12]{3,2,1,0:T(8,128)S(1)} %select_bitcast_fusion.2), custom_call_target="InvertDiagBlocksLowerTriangular" | custom-call | tf_op jit(solution)/shard_map/while/body/eval_jaxpr/triangular_solve | solution.py:64
  886.8 3.2 fusion.100
  891.1 17.6 %custom-call.12 = f32[16,12,12]{2,1,0:T(8,128)S(1)} custom-call(f32[16,12,12]{2,1,0:T(8,128)S(1)} %copy.101), custom_call_target="Cholesky" | custom-call | tf_op jit(solution)/shard_map/while/body/eval_jaxpr/jit(cholesky)/cholesky | solution.py:61
  909.0 14.9 %custom-call.13 = f32[16,1,12,12]{2,3,1,0:T(8,128)S(1)} custom-call(f32[16,1,12,12]{3,2,1,0:T(8,128)S(1)} %select_bitcast_fusion.2), custom_call_target="InvertDiagBlocksLowerTriangular" | custom-call | tf_op jit(solution)/shard_map/while/body/eval_jaxpr/triangular_solve | solution.py:64
  929.7 3.2 fusion.100
  934.0 17.6 %custom-call.12 = f32[16,12,12]{2,1,0:T(8,128)S(1)} custom-call(f32[16,12,12]{2,1,0:T(8,128)S(1)} %copy.101), custom_call_target="Cholesky" | custom-call | tf_op jit(solution)/shard_map/while/body/eval_jaxpr/jit(cholesky)/cholesky | solution.py:61
  951.9 14.9 %custom-call.13 = f32[16,1,12,12]{2,3,1,0:T(8,128)S(1)} custom-call(f32[16,1,12,12]{3,2,1,0:T(8,128)S(1)} %select_bitcast_fusion.2), custom_call_target="InvertDiagBlocksLowerTriangular" | custom-call | tf_op jit(solution)/shard_map/while/body/eval_jaxpr/triangular_solve | solution.py:64
  976.9 17.6 %custom-call.12 = f32[16,12,12]{2,1,0:T(8,128)S(1)} custom-call(f32[16,12,12]{2,1,0:T(8,128)S(1)} %copy.101), custom_call_target="Cholesky" | custom-call | tf_op jit(solution)/shard_map/while/body/eval_jaxpr/jit(cholesky)/cholesky | solution.py:61
  994.8 14.9 %custom-call.13 = f32[16,1,12,12]{2,3,1,0:T(8,128)S(1)} custom-call(f32[16,1,12,12]{3,2,1,0:T(8,128)S(1)} %select_bitcast_fusion.2), custom_call_target="InvertDiagBlocksLowerTriangular" | custom-call | tf_op jit(solution)/shard_map/while/body/eval_jaxpr/triangular_solve | solution.py:64
  1015.5 3.2 fusion.100
  1019.8 17.6 %custom-call.12 = f32[16,12,12]{2,1,0:T(8,128)S(1)} custom-call(f32[16,12,12]{2,1,0:T(8,128)S(1)} %copy.101), custom_call_target="Cholesky" | custom-call | tf_op jit(solution)/shard_map/while/body/eval_jaxpr/jit(cholesky)/cholesky | solution.py:61
  1037.7 14.9 %custom-call.13 = f32[16,1,12,12]{2,3,1,0:T(8,128)S(1)} custom-call(f32[16,1,12,12]{3,2,1,0:T(8,128)S(1)} %select_bitcast_fusion.2), custom_call_target="InvertDiagBlocksLowerTriangular" | custom-call | tf_op jit(solution)/shard_map/while/body/eval_jaxpr/triangular_solve | solution.py:64
  1058.4 3.2 fusion.100
  1062.7 17.6 %custom-call.12 = f32[16,12,12]{2,1,0:T(8,128)S(1)} custom-call(f32[16,12,12]{2,1,0:T(8,128)S(1)} %copy.101), custom_call_target="Cholesky" | custom-call | tf_op jit(solution)/shard_map/while/body/eval_jaxpr/jit(cholesky)/cholesky | solution.py:61
  1080.6 14.9 %custom-call.13 = f32[16,1,12,12]{2,3,1,0:T(8,128)S(1)} custom-call(f32[16,1,12,12]{3,2,1,0:T(8,128)S(1)} %select_bitcast_fusion.2), custom_call_target="InvertDiagBlocksLowerTriangular" | custom-call | tf_op jit(solution)/shard_map/while/body/eval_jaxpr/triangular_solve | solution.py:64
  1105.6 17.6 %custom-call.12 = f32[16,12,12]{2,1,0:T(8,128)S(1)} custom-call(f32[16,12,12]{2,1,0:T(8,128)S(1)} %copy.101), custom_call_target="Cholesky" | custom-call | tf_op jit(solution)/shard_map/while/body/eval_jaxpr/jit(cholesky)/cholesky | solution.py:61
  1123.5 14.9 %custom-call.13 = f32[16,1,12,12]{2,3,1,0:T(8,128)S(1)} custom-call(f32[16,1,12,12]{3,2,1,0:T(8,128)S(1)} %select_bitcast_fusion.2), custom_call_target="InvertDiagBlocksLowerTriangular" | custom-call | tf_op jit(solution)/shard_map/while/body/eval_jaxpr/triangular_solve | solution.py:64
  1144.2 3.2 fusion.100
  1148.5 17.6 %custom-call.12 = f32[16,12,12]{2,1,0:T(8,128)S(1)} custom-call(f32[16,12,12]{2,1,0:T(8,128)S(1)} %copy.101), custom_call_target="Cholesky" | custom-call | tf_op jit(solution)/shard_map/while/body/eval_jaxpr/jit(cholesky)/cholesky | solution.py:61
  1166.4 14.9 %custom-call.13 = f32[16,1,12,12]{2,3,1,0:T(8,128)S(1)} custom-call(f32[16,1,12,12]{3,2,1,0:T(8,128)S(1)} %select_bitcast_fusion.2), custom_call_target="InvertDiagBlocksLowerTriangular" | custom-call | tf_op jit(solution)/shard_map/while/body/eval_jaxpr/triangular_solve | solution.py:64
  1187.1 3.2 fusion.100
  1191.4 17.6 %custom-call.12 = f32[16,12,12]{2,1,0:T(8,128)S(1)} custom-call(f32[16,12,12]{2,1,0:T(8,128)S(1)} %copy.101), custom_call_target="Cholesky" | custom-call | tf_op jit(solution)/shard_map/while/body/eval_jaxpr/jit(cholesky)/cholesky | solution.py:61
  1209.3 14.9 %custom-call.13 = f32[16,1,12,12]{2,3,1,0:T(8,128)S(1)} custom-call(f32[16,1,12,12]{3,2,1,0:T(8,128)S(1)} %select_bitcast_fusion.2), custom_call_target="InvertDiagBlocksLowerTriangular" | custom-call | tf_op jit(solution)/shard_map/while/body/eval_jaxpr/triangular_solve | solution.py:64
  1234.3 17.6 %custom-call.12 = f32[16,12,12]{2,1,0:T(8,128)S(1)} custom-call(f32[16,12,12]{2,1,0:T(8,128)S(1)} %copy.101), custom_call_target="Cholesky" | custom-call | tf_op jit(solution)/shard_map/while/body/eval_jaxpr/jit(cholesky)/cholesky | solution.py:61
  1252.2 14.9 %custom-call.13 = f32[16,1,12,12]{2,3,1,0:T(8,128)S(1)} custom-call(f32[16,1,12,12]{3,2,1,0:T(8,128)S(1)} %select_bitcast_fusion.2), custom_call_target="InvertDiagBlocksLowerTriangular" | custom-call | tf_op jit(solution)/shard_map/while/body/eval_jaxpr/triangular_solve | solution.py:64
  1277.2 17.6 %custom-call.12 = f32[16,12,12]{2,1,0:T(8,128)S(1)} custom-call(f32[16,12,12]{2,1,0:T(8,128)S(1)} %copy.101), custom_call_target="Cholesky" | custom-call | tf_op jit(solution)/shard_map/while/body/eval_jaxpr/jit(cholesky)/cholesky | solution.py:61
  1295.1 14.9 %custom-call.13 = f32[16,1,12,12]{2,3,1,0:T(8,128)S(1)} custom-call(f32[16,1,12,12]{3,2,1,0:T(8,128)S(1)} %select_bitcast_fusion.2), custom_call_target="InvertDiagBlocksLowerTriangular" | custom-call | tf_op jit(solution)/shard_map/while/body/eval_jaxpr/triangular_solve | solution.py:64
  1315.8 3.2 fusion.100
  1320.1 17.6 %custom-call.12 = f32[16,12,12]{2,1,0:T(8,128)S(1)} custom-call(f32[16,12,12]{2,1,0:T(8,128)S(1)} %copy.101), custom_call_target="Cholesky" | custom-call | tf_op jit(solution)/shard_map/while/body/eval_jaxpr/jit(cholesky)/cholesky | solution.py:61
  1338.0 14.9 %custom-call.13 = f32[16,1,12,12]{2,3,1,0:T(8,128)S(1)} custom-call(f32[16,1,12,12]{3,2,1,0:T(8,128)S(1)} %select_bitcast_fusion.2), custom_call_target="InvertDiagBlocksLowerTriangular" | custom-call | tf_op jit(solution)/shard_map/while/body/eval_jaxpr/triangular_solve | solution.py:64
  1363.0 17.6 %custom-call.12 = f32[16,12,12]{2,1,0:T(8,128)S(1)} custom-call(f32[16,12,12]{2,1,0:T(8,128)S(1)} %copy.101), custom_call_target="Cholesky" | custom-call | tf_op jit(solution)/shard_map/while/body/eval_jaxpr/jit(cholesky)/cholesky | solution.py:61
  1380.9 14.9 %custom-call.13 = f32[16,1,12,12]{2,3,1,0:T(8,128)S(1)} custom-call(f32[16,1,12,12]{3,2,1,0:T(8,128)S(1)} %select_bitcast_fusion.2), custom_call_target="InvertDiagBlocksLowerTriangular" | custom-call | tf_op jit(solution)/shard_map/while/body/eval_jaxpr/triangular_solve | solution.py:64
  1405.9 17.6 %custom-call.12 = f32[16,12,12]{2,1,0:T(8,128)S(1)} custom-call(f32[16,12,12]{2,1,0:T(8,128)S(1)} %copy.101), custom_call_target="Cholesky" | custom-call | tf_op jit(solution)/shard_map/while/body/eval_jaxpr/jit(cholesky)/cholesky | solution.py:61
  1423.8 14.9 %custom-call.13 = f32[16,1,12,12]{2,3,1,0:T(8,128)S(1)} custom-call(f32[16,1,12,12]{3,2,1,0:T(8,128)S(1)} %select_bitcast_fusion.2), custom_call_target="InvertDiagBlocksLowerTriangular" | custom-call | tf_op jit(solution)/shard_map/while/body/eval_jaxpr/triangular_solve | solution.py:64
  (438 shorter events, 143.8 us)
Async XLA Ops:
  11.6 6.0 copy-start.1
  11.6 111.1 %all-to-all-start = ((bf16[3,2,384,1536]{3,0,1,2:T(4,128)(2,1)}), bf16[3,2,384,1536]{3,0,1,2:T(4,128)(2,1)}, u32[]{:S(2)}, u32[]{:S(2)}) async-start(bf16[3,2,384,1536]{3,0,1,2:T(4,128)(2,1)} %copy.69), calls=%async_computation | async-start | bytes 18874368 | tf_op jit(solution)/shard_map/all_to_all | solution.py:82
  226.7 145.1 %all-to-all-start.1 = ((f32[12,2,512,96]{3,1,0,2:T(2,128)}), f32[12,2,512,96]{3,1,0,2:T(2,128)}, u32[]{:S(2)}, u32[]{:S(2)}) async-start(f32[12,2,512,96]{3,1,0,2:T(2,128)} %copy.74), calls=%async_computation.1 | async-start | bytes 12582912 | tf_op jit(solution)/shard_map/all_to_all | solution.py:93
  486.8 126.1 %copy-start = (f32[3072,128]{1,0:T(8,128)S(1)}, f32[3072,128]{1,0:T(8,128)}, u32[]{:S(2)}) copy-start(f32[3072,128]{1,0:T(8,128)} %fusion.74) | copy-start | bytes 4718596
where the time goes:
time: 1450 us; the launch traced here: 1440 us
  other arithmetic  690 us (48%)
  matrix products  390 us (27%)
  waiting for transfers between devices  224 us (15%)
  local copies, waits for them, and re-layouts  126 us (9%)
    another operation x64, other arithmetic, cycle_combine(): factor = jnp.linalg.cholesky(regular)  284 us
    another operation x48, other arithmetic, cycle_combine(): lax.linalg.triangular_solve(factor, forward, left_side=True, lower=True,...  240 us
    dot_general x1, matrix products, cycle_synthesis(): jnp.dot(shifted_real, fine_cos, precision=highest, preferred_element_type...  126 us
    dot_general x1, matrix products, cycle_synthesis(): jnp.dot(shifted_imag, fine_sin, precision=highest, preferred_element_type...  125 us
    all_to_all x1, waiting for transfers between devices, per_device(): lax.all_to_all(spectra, ('chan', 'blk'), split_axis=2, concat_axis=3, til...  119 us
    all_to_all x1, waiting for transfers between devices, per_device(): lax.all_to_all(coeffs, 'chan', split_axis=2, concat_axis=0, tiled=True)  105 us
    add x1, other arithmetic, cycle_synthesis(): real_part * coarse_sin[None] + imag_part * coarse_cos[None]  95.4 us
    dot_general x16, matrix products, cycle_combine(): moments = jnp.einsum('qx,kx->kq', products, member, precision=highest)  51.2 us
  transfers between devices with their start and end apart: 2, of which 2 were waited for; matrix products, arithmetic and copies ran while one was open for 1% of the time, Pallas kernels for 0%

commit v1 on v0

--- a/solution.py
+++ b/solution.py
@@ -70,6 +70,19 @@
 
 
 def per_device(coeffs, legendre, m_order, sector_len):
+
+    def points_post(my_data):
+        d_next = jnp.concatenate(
+            lax.all_to_all(
+                jnp.stack(jnp.split(my_data, lax.axis_size(("chan", "blk")), 2), axis=0),
+                ("chan", "blk"),
+                split_axis=0,
+                concat_axis=0,
+            ),
+            3,
+        )
+        return d_next
+
     slot_count = legendre.shape[1]
     group_count = lax.axis_size("chan")
     block_count = lax.axis_size("blk")
@@ -89,9 +102,7 @@
     order_joined = (
         m_order.reshape(block_count, group_count, slot_count).transpose(1, 0, 2).reshape(-1)
     )
-    cycle_maps = (lambda spectrum: cycle_synthesis(spectrum, order_joined))(
-        lax.all_to_all(spectra, ("chan", "blk"), split_axis=2, concat_axis=3, tiled=True)
-    )
+    cycle_maps = (lambda spectrum: cycle_synthesis(spectrum, order_joined))(points_post(spectra))
     return lax.map(
         lambda cycle_pair: cycle_combine(cycle_pair[0], cycle_pair[1]),
         (jnp.moveaxis(cycle_maps, 1, 0), sector_len),

time: 1450 us -> 1590 us (1.097)
  local copies, waits for them, and re-layouts: 126 us -> 268 us
    another operation x32 -> x67, local copies, waits for them, and re-layouts: 1.38 us -> 120 us  [the longest x35 119 us: points_post(): jnp.stack(jnp.split(my_data, lax.axis_size(('chan', 'blk')), 2), axis=0)]
    unnamed x5 -> x74, local copies, waits for them, and re-layouts: 11.6 us -> 45.3 us
    reshape x0 -> x2, local copies, waits for them, and re-layouts: none -> 16.7 us  [points_post(): jnp.concatenate(lax.all_to_all(jnp.stack(jnp.split(my_data, lax.axis_size...]
    all_to_all x3 -> x0, local copies, waits for them, and re-layouts: 16.7 us -> none  [per_device(): lax.all_to_all(spectra, ('chan', 'blk'), split_axis=2, concat_axis=3, til...]
where the time goes in v1:
time: 1590 us; the launch traced here: 1580 us
  other arithmetic  683 us (43%)
  matrix products  387 us (24%)
  local copies, waits for them, and re-layouts  268 us (17%)
  waiting for transfers between devices  224 us (14%)
    another operation x64, other arithmetic, cycle_combine(): factor = jnp.linalg.cholesky(regular)  284 us
    another operation x48, other arithmetic, cycle_combine(): lax.linalg.triangular_solve(factor, forward, left_side=True, lower=True,...  240 us
    dot_general x1, matrix products, cycle_synthesis(): jnp.dot(shifted_real, fine_cos, precision=highest, preferred_element_type...  126 us
    dot_general x1, matrix products, cycle_synthesis(): jnp.dot(shifted_imag, fine_sin, precision=highest, preferred_element_type...  125 us
    all_to_all x1, waiting for transfers between devices, points_post(): lax.all_to_all(jnp.stack(jnp.split(my_data, lax.axis_size(('chan', 'blk')...  119 us
    another operation x35, local copies, waits for them, and re-layouts, points_post(): jnp.stack(jnp.split(my_data, lax.axis_size(('chan', 'blk')), 2), axis=0)  119 us
    all_to_all x1, waiting for transfers between devices, per_device(): lax.all_to_all(coeffs, 'chan', split_axis=2, concat_axis=0, tiled=True)  104 us
    add x1, other arithmetic, cycle_synthesis(): real_part * coarse_sin[None] + imag_part * coarse_cos[None]  95.4 us
  transfers between devices with their start and end apart: 2, of which 2 were waited for; matrix products, arithmetic and copies ran while one was open for 1% of the time, Pallas kernels for 0%

profile of v1, /device:TPU:0, one launch (start us, length us, event | category | flops | bytes accessed | tf_op | source)
XLA Modules:
  0.0 1576.1 jit_solution(16239727196051832581)
XLA Ops:
  0.0 11.6 copy.131
  11.6 5.9 all-to-all-start
  18.2 104.5 %all-to-all-done = bf16[3,2,384,1536]{3,0,1,2:T(4,128)(2,1)} async-done(((bf16[3,2,384,1536]{3,0,1,2:T(4,128)(2,1)}), bf16[3,2,384,1536]{3,0,1,2:T(4,128)(2,1)}, u32[]{:S(2)}, u32[]{:S(2)}) %all-to-all-start) | async-done | bytes 7077920 | tf_op jit(solution)/shard_map/all_to_all | solution.py:95
  122.7 6.5 copy.132
  129.2 3.3 copy.133
  132.5 10.2 bitcast_select_fusion
  142.6 32.4 %fusion.23 = f32[96,12,2,256]{3,1,2,0:T(8,128)} fusion(bf16[1,96,256,1536]{3,2,1,0:T(8,128)(2,1)} %param.7, bf16[12,2,96,1536]{3,2,1,0:T(8,128)(2,1)} %get-tuple-element.40), kind=kOutput, calls=%fused_computation.41 | convolution fusion | flops 1811939328 | bytes 84934656 | tf_op jit(solution)/shard_map/cpsl,srl->cprs/dot_general | solution.py:100
  175.0 32.9 %subtract_bitcast_fusion = (f32[12,2,256,96]{2,0,1,3:T(8,128)S(1)}, f32[12,2,256,96]{2,0,1,3:T(8,128)}) fusion(f32[96,12,2,256]{3,1,2,0:T(8,128)} %fusion.23, bf16[1,96,256,1536]{3,2,1,0:T(8,128)(2,1)} %param.7, bf16[12,2,96,1536]{3,2,1,0:T(8,128)(2,1)} %get-tuple-element.41), kind=kOutput, calls=%fused_computation.51 | convolution fusion | flops 1813118976 | bytes 89653248 | tf_op jit(solution)/shard_map/cpsl,srl->cprs/dot_general | solution.py:99
  208.0 27.7 %slice_bitcast_fusion.16 = (f32[1,12,2,16,96]{3,1,2,4,0:T(8,128)}, f32[1,12,2,16,96]{3,1,2,4,0:T(8,128)}, f32[1,12,2,16,96]{3,1,2,4,0:T(8,128)}, f32[1,12,2,16,9...) fusion(f32[12,2,256,96]{2,0,1,3:T(8,128)} %get-tuple-element.45), kind=kLoop, calls=%fused_computation.75 | loop fusion | bytes 4718592 | tf_op jit(solution)/shard_map/stack | solution.py:77
  277.5 11.5 slice_bitcast_fusion
  360.4 5.6 all-to-all-start.1
  366.2 4.2 fusion.50
  370.4 8.1 fusion.76
  378.4 8.1 fusion.74
  386.5 119.3 %all-to-all-done.1 = f32[32,12,2,16,96]{4,3,2,1,0:T(8,128)} async-done(((f32[32,12,2,16,96]{4,3,2,1,0:T(8,128)}), f32[32,12,2,16,96]{4,3,2,1,0:T(8,128)}, u32[]{:S(2)}, u32[]{:S(2)}) %all-to-all-start.1) | async-done | bytes 4718624 | tf_op jit(solution)/shard_map/all_to_all | solution.py:76
  505.9 9.1 copy.168
  514.9 7.7 reshape.302
  525.5 95.4 %multiply_add_fusion = (f32[192,64,3072]{2,1,0:T(8,128)}, f32[192,64,3072]{2,1,0:T(8,128)}) fusion(f32[64,3072]{1,0:T(8,128)} %get-tuple-element.81, f32[192,3072]{1,0:T(8,128)S(1)} %bitcast.169, f32[64,3072]{1,0:T(8,128)} %get-tuple-element.80, f32[192,3072]{1,0:T(8,128)S(1)} %bitcast.168), kind=kLoop, calls=%fused_computation.39 | loop fusion | flops 226492416 | bytes 308281344 | tf_op jit(solution)/shard_map/add | solution.py:32
  621.0 126.1 %fusion.34 = f32[12288,128]{1,0:T(8,128)} fusion(f32[12288,3072]{1,0:T(8,128)} %bitcast.60, f32[3072,128]{1,0:T(8,128)} %fusion.76), kind=kOutput, calls=%fused_computation.93 | convolution fusion | flops 57982058496 | bytes 158859264 | tf_op jit(solution)/shard_map/dot_general | solution.py:35
  747.0 125.4 %convolution_subtract_fusion = f32[12288,128]{1,0:T(8,128)} fusion(f32[12288,128]{1,0:T(8,128)} %fusion.34, f32[12288,3072]{1,0:T(8,128)} %bitcast.61, f32[3072,128]{1,0:T(8,128)S(1)} %copy-done), kind=kOutput, calls=%fused_computation.45 | convolution fusion | flops 57983631360 | bytes 165150720 | tf_op jit(solution)/shard_map/dot_general | solution.py:36
  872.4 7.4 reshape.304
  879.8 9.7 copy.183
  889.5 686.4 %while.10 = (s32[]{:T(128)}, f32[16,8192]{1,0:T(8,128)}, s32[16,16]{1,0:T(8,128)}, f32[16,12,8192]{2,1,0:T(8,128)}, s32[]{:T(128)}, /*index=5*/s32[]{:T(128)}, f32[]{:T(128)}, f32[]{:T(128)}) while((s32[]{:T(128)}, f32[16,8192]{1,0:T(8,128)}, s32[16,16]{1,0:T(8,128)}, f32[16,12,8192]{2,1,0:T(8,128)}, s32[]{:T(128)}, /*index=5*/s32[]{:T(128)}, ...), condition=%wide.region_7.8_spmd, body=%wide.region_0.7_spmd.sunk | while | flops 247610512 | bytes 1840549 | solution.py:106
  892.2 3.2 fusion.100
  896.5 17.6 %custom-call.14 = f32[16,12,12]{2,1,0:T(8,128)S(1)} custom-call(f32[16,12,12]{2,1,0:T(8,128)S(1)} %copy.193), custom_call_target="Cholesky" | custom-call | tf_op jit(solution)/shard_map/while/body/eval_jaxpr/jit(cholesky)/cholesky | solution.py:61
  914.4 14.9 custom-call.15
  939.4 17.6 %custom-call.14 = f32[16,12,12]{2,1,0:T(8,128)S(1)} custom-call(f32[16,12,12]{2,1,0:T(8,128)S(1)} %copy.193), custom_call_target="Cholesky" | custom-call | tf_op jit(solution)/shard_map/while/body/eval_jaxpr/jit(cholesky)/cholesky | solution.py:61
  957.3 14.9 custom-call.15
  978.0 3.2 fusion.100
  982.3 17.6 %custom-call.14 = f32[16,12,12]{2,1,0:T(8,128)S(1)} custom-call(f32[16,12,12]{2,1,0:T(8,128)S(1)} %copy.193), custom_call_target="Cholesky" | custom-call | tf_op jit(solution)/shard_map/while/body/eval_jaxpr/jit(cholesky)/cholesky | solution.py:61
  1000.2 14.9 custom-call.15
  1025.2 17.6 %custom-call.14 = f32[16,12,12]{2,1,0:T(8,128)S(1)} custom-call(f32[16,12,12]{2,1,0:T(8,128)S(1)} %copy.193), custom_call_target="Cholesky" | custom-call | tf_op jit(solution)/shard_map/while/body/eval_jaxpr/jit(cholesky)/cholesky | solution.py:61
  1043.1 14.9 custom-call.15
  1063.8 3.2 fusion.100
  1068.1 17.6 %custom-call.14 = f32[16,12,12]{2,1,0:T(8,128)S(1)} custom-call(f32[16,12,12]{2,1,0:T(8,128)S(1)} %copy.193), custom_call_target="Cholesky" | custom-call | tf_op jit(solution)/shard_map/while/body/eval_jaxpr/jit(cholesky)/cholesky | solution.py:61
  1086.0 14.9 custom-call.15
  1106.7 3.2 fusion.100
  1111.0 17.6 %custom-call.14 = f32[16,12,12]{2,1,0:T(8,128)S(1)} custom-call(f32[16,12,12]{2,1,0:T(8,128)S(1)} %copy.193), custom_call_target="Cholesky" | custom-call | tf_op jit(solution)/shard_map/while/body/eval_jaxpr/jit(cholesky)/cholesky | solution.py:61
  1128.9 14.9 custom-call.15
  1153.9 17.6 %custom-call.14 = f32[16,12,12]{2,1,0:T(8,128)S(1)} custom-call(f32[16,12,12]{2,1,0:T(8,128)S(1)} %copy.193), custom_call_target="Cholesky" | custom-call | tf_op jit(solution)/shard_map/while/body/eval_jaxpr/jit(cholesky)/cholesky | solution.py:61
  1171.8 14.9 custom-call.15
  1192.5 3.2 fusion.100
  1196.8 17.6 %custom-call.14 = f32[16,12,12]{2,1,0:T(8,128)S(1)} custom-call(f32[16,12,12]{2,1,0:T(8,128)S(1)} %copy.193), custom_call_target="Cholesky" | custom-call | tf_op jit(solution)/shard_map/while/body/eval_jaxpr/jit(cholesky)/cholesky | solution.py:61
  1214.7 14.9 custom-call.15
  1235.4 3.2 fusion.100
  1239.7 17.6 %custom-call.14 = f32[16,12,12]{2,1,0:T(8,128)S(1)} custom-call(f32[16,12,12]{2,1,0:T(8,128)S(1)} %copy.193), custom_call_target="Cholesky" | custom-call | tf_op jit(solution)/shard_map/while/body/eval_jaxpr/jit(cholesky)/cholesky | solution.py:61
  1257.6 14.9 custom-call.15
  1282.6 17.6 %custom-call.14 = f32[16,12,12]{2,1,0:T(8,128)S(1)} custom-call(f32[16,12,12]{2,1,0:T(8,128)S(1)} %copy.193), custom_call_target="Cholesky" | custom-call | tf_op jit(solution)/shard_map/while/body/eval_jaxpr/jit(cholesky)/cholesky | solution.py:61
  1300.5 14.9 custom-call.15
  1321.2 3.2 fusion.100
  1325.5 17.6 %custom-call.14 = f32[16,12,12]{2,1,0:T(8,128)S(1)} custom-call(f32[16,12,12]{2,1,0:T(8,128)S(1)} %copy.193), custom_call_target="Cholesky" | custom-call | tf_op jit(solution)/shard_map/while/body/eval_jaxpr/jit(cholesky)/cholesky | solution.py:61
  1343.4 14.9 custom-call.15
  1364.1 3.2 fusion.100
  1368.4 17.6 %custom-call.14 = f32[16,12,12]{2,1,0:T(8,128)S(1)} custom-call(f32[16,12,12]{2,1,0:T(8,128)S(1)} %copy.193), custom_call_target="Cholesky" | custom-call | tf_op jit(solution)/shard_map/while/body/eval_jaxpr/jit(cholesky)/cholesky | solution.py:61
  1386.3 14.9 custom-call.15
  1411.3 17.6 %custom-call.14 = f32[16,12,12]{2,1,0:T(8,128)S(1)} custom-call(f32[16,12,12]{2,1,0:T(8,128)S(1)} %copy.193), custom_call_target="Cholesky" | custom-call | tf_op jit(solution)/shard_map/while/body/eval_jaxpr/jit(cholesky)/cholesky | solution.py:61
  1429.2 14.9 custom-call.15
  1449.9 3.2 fusion.100
  1454.2 17.6 %custom-call.14 = f32[16,12,12]{2,1,0:T(8,128)S(1)} custom-call(f32[16,12,12]{2,1,0:T(8,128)S(1)} %copy.193), custom_call_target="Cholesky" | custom-call | tf_op jit(solution)/shard_map/while/body/eval_jaxpr/jit(cholesky)/cholesky | solution.py:61
  1472.1 14.9 custom-call.15
  1497.1 17.6 %custom-call.14 = f32[16,12,12]{2,1,0:T(8,128)S(1)} custom-call(f32[16,12,12]{2,1,0:T(8,128)S(1)} %copy.193), custom_call_target="Cholesky" | custom-call | tf_op jit(solution)/shard_map/while/body/eval_jaxpr/jit(cholesky)/cholesky | solution.py:61
  1514.9 14.9 custom-call.15
  1540.0 17.6 %custom-call.14 = f32[16,12,12]{2,1,0:T(8,128)S(1)} custom-call(f32[16,12,12]{2,1,0:T(8,128)S(1)} %copy.193), custom_call_target="Cholesky" | custom-call | tf_op jit(solution)/shard_map/while/body/eval_jaxpr/jit(cholesky)/cholesky | solution.py:61
  1557.8 14.9 custom-call.15
  (539 shorter events, 253.6 us)
Async XLA Ops:
  11.6 6.0 copy-start.20
  11.6 111.1 %all-to-all-start = ((bf16[3,2,384,1536]{3,0,1,2:T(4,128)(2,1)}), bf16[3,2,384,1536]{3,0,1,2:T(4,128)(2,1)}, u32[]{:S(2)}, u32[]{:S(2)}) async-start(bf16[3,2,384,1536]{3,0,1,2:T(4,128)(2,1)} %copy.131), calls=%async_computation | async-start | bytes 18874368 | tf_op jit(solution)/shard_map/all_to_all | solution.py:95
  289.0 16.4 %copy-start.4 = (f32[1,12,2,16,96]{3,1,2,4,0:T(8,128)S(1)}, f32[1,12,2,16,96]{3,1,2,4,0:T(8,128)}, u32[]{:S(2)}) copy-start(f32[1,12,2,16,96]{3,1,2,4,0:T(8,128)} %get-tuple-element.57) | copy-start | bytes 442372
  289.0 17.8 %copy-start.3 = (f32[1,12,2,16,96]{3,1,2,4,0:T(8,128)S(1)}, f32[1,12,2,16,96]{3,1,2,4,0:T(8,128)}, u32[]{:S(2)}) copy-start(f32[1,12,2,16,96]{3,1,2,4,0:T(8,128)} %get-tuple-element.56) | copy-start | bytes 442372
  306.8 17.7 %copy-start.2 = (f32[1,12,2,16,96]{3,1,2,4,0:T(8,128)S(1)}, f32[1,12,2,16,96]{3,1,2,4,0:T(8,128)}, u32[]{:S(2)}) copy-start(f32[1,12,2,16,96]{3,1,2,4,0:T(8,128)} %get-tuple-element.49) | copy-start | bytes 442372
  308.2 17.8 %copy-start.1 = (f32[1,12,2,16,96]{3,1,2,4,0:T(8,128)S(1)}, f32[1,12,2,16,96]{3,1,2,4,0:T(8,128)}, u32[]{:S(2)}) copy-start(f32[1,12,2,16,96]{3,1,2,4,0:T(8,128)} %get-tuple-element.48) | copy-start | bytes 442372
  325.9 20.4 %copy-start.5 = (f32[1,12,2,16,96]{4,3,2,1,0:T(8,128)S(1)}, f32[1,12,2,16,96]{4,3,2,1,0:T(8,128)}, u32[]{:S(2)}) copy-start(f32[1,12,2,16,96]{4,3,2,1,0:T(8,128)} %copy.149) | copy-start | bytes 442372
  325.9 29.6 %copy-start.11 = (f32[1,12,2,16,96]{4,3,2,1,0:T(8,128)S(1)}, f32[1,12,2,16,96]{4,3,2,1,0:T(8,128)}, u32[]{:S(2)}) copy-start(f32[1,12,2,16,96]{4,3,2,1,0:T(8,128)} %copy.161) | copy-start | bytes 442372
  325.9 30.3 %copy-start.10 = (f32[1,12,2,16,96]{4,3,2,1,0:T(8,128)S(1)}, f32[1,12,2,16,96]{4,3,2,1,0:T(8,128)}, u32[]{:S(2)}) copy-start(f32[1,12,2,16,96]{4,3,2,1,0:T(8,128)} %copy.162) | copy-start | bytes 442372
  325.9 31.0 %copy-start.9 = (f32[1,12,2,16,96]{4,3,2,1,0:T(8,128)S(1)}, f32[1,12,2,16,96]{4,3,2,1,0:T(8,128)}, u32[]{:S(2)}) copy-start(f32[1,12,2,16,96]{4,3,2,1,0:T(8,128)} %copy.163) | copy-start | bytes 442372
  325.9 31.7 %copy-start.8 = (f32[1,12,2,16,96]{4,3,2,1,0:T(8,128)S(1)}, f32[1,12,2,16,96]{4,3,2,1,0:T(8,128)}, u32[]{:S(2)}) copy-start(f32[1,12,2,16,96]{4,3,2,1,0:T(8,128)} %copy.164) | copy-start | bytes 442372
  325.9 32.4 %copy-start.7 = (f32[1,12,2,16,96]{4,3,2,1,0:T(8,128)S(1)}, f32[1,12,2,16,96]{4,3,2,1,0:T(8,128)}, u32[]{:S(2)}) copy-start(f32[1,12,2,16,96]{4,3,2,1,0:T(8,128)} %copy.165) | copy-start | bytes 442372
  325.9 33.1 %copy-start.6 = (f32[1,12,2,16,96]{4,3,2,1,0:T(8,128)S(1)}, f32[1,12,2,16,96]{4,3,2,1,0:T(8,128)}, u32[]{:S(2)}) copy-start(f32[1,12,2,16,96]{4,3,2,1,0:T(8,128)} %copy.166) | copy-start | bytes 442372
  326.7 23.3 %copy-start.19 = (f32[1,12,2,16,96]{4,3,2,1,0:T(8,128)S(1)}, f32[1,12,2,16,96]{4,3,2,1,0:T(8,128)}, u32[]{:S(2)}) copy-start(f32[1,12,2,16,96]{4,3,2,1,0:T(8,128)} %copy.153) | copy-start | bytes 442372
  326.7 24.0 %copy-start.18 = (f32[1,12,2,16,96]{4,3,2,1,0:T(8,128)S(1)}, f32[1,12,2,16,96]{4,3,2,1,0:T(8,128)}, u32[]{:S(2)}) copy-start(f32[1,12,2,16,96]{4,3,2,1,0:T(8,128)} %copy.154) | copy-start | bytes 442372
  326.7 24.7 %copy-start.17 = (f32[1,12,2,16,96]{4,3,2,1,0:T(8,128)S(1)}, f32[1,12,2,16,96]{4,3,2,1,0:T(8,128)}, u32[]{:S(2)}) copy-start(f32[1,12,2,16,96]{4,3,2,1,0:T(8,128)} %copy.155) | copy-start | bytes 442372
  326.7 25.3 %copy-start.16 = (f32[1,12,2,16,96]{4,3,2,1,0:T(8,128)S(1)}, f32[1,12,2,16,96]{4,3,2,1,0:T(8,128)}, u32[]{:S(2)}) copy-start(f32[1,12,2,16,96]{4,3,2,1,0:T(8,128)} %copy.156) | copy-start | bytes 442372
  326.7 26.0 %copy-start.15 = (f32[1,12,2,16,96]{4,3,2,1,0:T(8,128)S(1)}, f32[1,12,2,16,96]{4,3,2,1,0:T(8,128)}, u32[]{:S(2)}) copy-start(f32[1,12,2,16,96]{4,3,2,1,0:T(8,128)} %copy.157) | copy-start | bytes 442372
  326.7 26.7 %copy-start.14 = (f32[1,12,2,16,96]{4,3,2,1,0:T(8,128)S(1)}, f32[1,12,2,16,96]{4,3,2,1,0:T(8,128)}, u32[]{:S(2)}) copy-start(f32[1,12,2,16,96]{4,3,2,1,0:T(8,128)} %copy.158) | copy-start | bytes 442372
  326.7 27.4 %copy-start.13 = (f32[1,12,2,16,96]{4,3,2,1,0:T(8,128)S(1)}, f32[1,12,2,16,96]{4,3,2,1,0:T(8,128)}, u32[]{:S(2)}) copy-start(f32[1,12,2,16,96]{4,3,2,1,0:T(8,128)} %copy.159) | copy-start | bytes 442372
  326.7 28.1 %copy-start.12 = (f32[1,12,2,16,96]{4,3,2,1,0:T(8,128)S(1)}, f32[1,12,2,16,96]{4,3,2,1,0:T(8,128)}, u32[]{:S(2)}) copy-start(f32[1,12,2,16,96]{4,3,2,1,0:T(8,128)} %copy.160) | copy-start | bytes 442372
  360.4 145.5 %all-to-all-start.1 = ((f32[32,12,2,16,96]{4,3,2,1,0:T(8,128)}), f32[32,12,2,16,96]{4,3,2,1,0:T(8,128)}, u32[]{:S(2)}, u32[]{:S(2)}) async-start(f32[32,12,2,16,96]{4,3,2,1,0:T(8,128)} %constant_dynamic-update-slice_fusion), calls=%async_computation.1 | async-start | bytes 12582912 | tf_op jit(solution)/shard_map/all_to_all | solution.py:76
  620.9 126.1 %copy-start = (f32[3072,128]{1,0:T(8,128)S(1)}, f32[3072,128]{1,0:T(8,128)}, u32[]{:S(2)}) copy-start(f32[3072,128]{1,0:T(8,128)} %fusion.74) | copy-start | bytes 4718596
